TPU v7x, 256 devices: a whole 4x4x8 slice. The times are simulated.
256 devices in a mesh: dp: 32 (over y, z), segment: 2 (over x_lo), chan: 4 (over x_hi, core).
Axes of the slice: x: 4 (x_hi: 2, x_lo: 2; x = x_hi * 2 + x_lo), y: 4, z: 8, core: 2. Of those that a mesh axis runs over, the one named last changes fastest.
Arguments:
- base: bfloat16 [64, 512, 256], P('dp', 'chan'), may hold values from -6 to 6
- style: float32 [2, 64, 512], P('segment', 'dp'), may hold values from -3 to 3
- noise: float32 [2, 64, 256], P('segment', 'dp'), may hold values from -6 to 6
- conv_weight: bfloat16 [2, 4608, 512], P('segment', None, 'chan'), may hold values from -0.09375 to 0.09375
- conv_bias: float32 [2, 512], P('segment', 'chan'), may hold values from -3 to 3
- noise_gain: float32 [2, 512], P('segment', 'chan'), may hold values from 0.1 to 1
- rgb_weight: bfloat16 [2, 3, 512], P('segment', None, 'chan'), may hold values from -0.25 to 0.25
- disc_weight: float32 [3, 256], replicated, may hold values from -3.5 to 3.5
- disc_bias: float32 [256], replicated, may hold values from -3 to 3
- disc_out: float32 [256], replicated, may hold values from -3 to 3
Outputs:
- conv_grad: float32 [2, 4608, 512], P('segment', 'dp', 'chan')
- logits: float32 [64], P('dp')
- section_input_grads: bfloat16 [2, 64, 512, 256], P('segment', 'dp', 'chan')
All inputs are finite; a program needn't handle non-finite values.
Results may differ from a plain program's by a relative error of at most 0.015.
Values may be sent and summed in bfloat16 or wider, within the bound.
No kernel may reach another device: no remote copies, remote signals or barrier semaphores. Data moves between devices by JAX's collectives and lax.ppermute only.
A program may use at most 64 MiB of HBM per device.

v0:
```python
import jax
import jax.numpy as jnp
from jax import lax
from jax.sharding import PartitionSpec as P

RES = 16
epsilon = 1e-06
root_two = 1.4142135623730951
highest = lax.Precision.HIGHEST
kernel_offsets = [(ky - 1, kx - 1) for ky in range(3) for kx in range(3)]


def shifted(value, axis, steps):
    count = lax.axis_size(axis)
    first, last = (max(0, -steps), min(count, count - steps))
    return lax.ppermute(value, axis, [(source, source + steps) for source in range(first, last)])


def leaky_relu(values):
    return 0.2 * values + 0.8 * jax.nn.softplus(values)


def leaky_slope(values):
    return 0.2 + 0.8 * jax.nn.sigmoid(values)


def shift_grid(values, offset_y, offset_x):
    leading = values.shape[:-1]
    planes = values.reshape(leading + (RES, RES))
    padded = jnp.pad(planes, [(0, 0)] * len(leading) + [(1, 1), (1, 1)])
    moved = padded[..., 1 + offset_y : 1 + offset_y + RES, 1 + offset_x : 1 + offset_x + RES]
    return moved.reshape(leading + (RES * RES,))


def store_slot(buffer, item, slot_clip, is_valid, axis_pos, width):
    offset = slot_clip * width
    previous = lax.dynamic_slice_in_dim(buffer, offset, width, axis_pos)
    return lax.dynamic_update_slice_in_dim(
        buffer, jnp.where(is_valid, item, previous), offset, axis_pos
    )


def shards(
    base,
    style,
    noise,
    conv_weight,
    conv_bias,
    noise_gain,
    rgb_weight,
    disc_weight,
    disc_bias,
    disc_out,
):
    weight = conv_weight[0]
    full_width = weight.shape[0] // 9
    own_width = weight.shape[1]
    micro_count = base.shape[0]
    pixels = base.shape[2]
    segment_index = lax.axis_index("segment")
    chan_index = lax.axis_index("chan")
    styles = style[0]
    own_styles = lax.dynamic_slice_in_dim(styles, chan_index * own_width, own_width, 1)
    w_float = weight.astype(jnp.float32)
    squares = jnp.sum((w_float * w_float).reshape(9, full_width, own_width), axis=0)
    style_sq = styles * styles
    demods = lax.rsqrt(
        jnp.dot(style_sq, squares, precision=highest, preferred_element_type=jnp.float32) + epsilon
    )
    bias_row = conv_bias[0]
    gain_row = noise_gain[0]
    noises = noise[0]
    rgb_proj = rgb_weight[0]
    columns_all = jnp.zeros((9 * full_width, micro_count * pixels), jnp.bfloat16)
    pre_all = jnp.zeros((micro_count, own_width, pixels), jnp.float32)
    conv_all = jnp.zeros((micro_count, own_width, pixels), jnp.float32)
    image_part = jnp.zeros((micro_count, 3, pixels), jnp.float32)
    outgoing = jnp.zeros((own_width, pixels), jnp.bfloat16)
    for tick_index in range(micro_count + 1):
        slot_index = tick_index - segment_index
        is_valid = (slot_index >= 0) & (slot_index < micro_count)
        slot_clip = jnp.clip(slot_index, 0, micro_count - 1)
        if tick_index > 0:
            incoming = shifted(outgoing, "segment", 1)
        else:
            incoming = outgoing
        first_input = lax.dynamic_index_in_dim(base, slot_clip, 0, keepdims=False)
        inputs = jnp.where(segment_index == 0, first_input, incoming)
        style_row = lax.dynamic_index_in_dim(own_styles, slot_clip, 0, keepdims=False)
        demod_row = lax.dynamic_index_in_dim(demods, slot_clip, 0, keepdims=False)
        noise_row = lax.dynamic_index_in_dim(noises, slot_clip, 0, keepdims=False)
        modulated = (inputs.astype(jnp.float32) * style_row[:, None]).astype(jnp.bfloat16)
        gathered = lax.all_gather(modulated, "chan", axis=0, tiled=True)
        columns = jnp.concatenate(
            [shift_grid(gathered, oy, ox) for oy, ox in kernel_offsets], axis=0
        )
        conv_out = lax.dot_general(
            weight, columns, (((0,), (0,)), ((), ())), preferred_element_type=jnp.float32
        )
        pre_act = (
            demod_row[:, None] * conv_out
            + gain_row[:, None] * noise_row[None, :]
            + bias_row[:, None]
        )
        out_act = (root_two * leaky_relu(pre_act)).astype(jnp.bfloat16)
        rgb_part = jnp.dot(rgb_proj, out_act, preferred_element_type=jnp.float32)
        columns_all = store_slot(columns_all, columns, slot_clip, is_valid, 1, pixels)
        pre_all = store_slot(pre_all, pre_act[None], slot_clip, is_valid, 0, 1)
        conv_all = store_slot(conv_all, conv_out[None], slot_clip, is_valid, 0, 1)
        image_part = store_slot(image_part, rgb_part[None], slot_clip, is_valid, 0, 1)
        outgoing = out_act
    images = lax.psum(image_part, ("segment", "chan"))
    pre_disc = (
        jnp.einsum("cj,mcp->mjp", disc_weight, images, precision=highest) + disc_bias[None, :, None]
    )
    hidden = leaky_relu(pre_disc)
    logits = jnp.dot(
        jnp.mean(hidden, axis=2), disc_out, precision=highest, preferred_element_type=jnp.float32
    )
    grad_logit = jax.nn.sigmoid(logits) - 1.0
    d_pre = grad_logit[:, None, None] * disc_out[None, :, None] / pixels * leaky_slope(pre_disc)
    d_image = jnp.einsum("cj,mjp->mcp", disc_weight, d_pre, precision=highest)
    head_grad = jnp.einsum("co,mcp->mop", rgb_proj.astype(jnp.float32), d_image, precision=highest)
    grads_all = jnp.zeros((own_width, micro_count * pixels), jnp.bfloat16)
    coef_all = jnp.zeros((micro_count, own_width), jnp.float32)
    returned_all = jnp.zeros((micro_count, own_width, pixels), jnp.bfloat16)
    returned = jnp.zeros((own_width, pixels), jnp.bfloat16)
    for tick_index in range(micro_count + 1):
        slot_index = tick_index - 1 + segment_index
        is_valid = (slot_index >= 0) & (slot_index < micro_count)
        slot_clip = jnp.clip(slot_index, 0, micro_count - 1)
        if tick_index > 0:
            incoming = shifted(returned, "segment", -1)
        else:
            incoming = returned
        style_row = lax.dynamic_index_in_dim(own_styles, slot_clip, 0, keepdims=False)
        demod_row = lax.dynamic_index_in_dim(demods, slot_clip, 0, keepdims=False)
        pre_act = lax.dynamic_index_in_dim(pre_all, slot_clip, 0, keepdims=False)
        conv_out = lax.dynamic_index_in_dim(conv_all, slot_clip, 0, keepdims=False)
        grad_out = lax.dynamic_index_in_dim(
            head_grad, slot_clip, 0, keepdims=False
        ) + incoming.astype(jnp.float32)
        d_act = grad_out * root_two * leaky_slope(pre_act)
        d_conv = (d_act * demod_row[:, None]).astype(jnp.bfloat16)
        d_demod = jnp.sum(d_act * conv_out, axis=1)
        coef_row = -d_demod * demod_row * demod_row * demod_row
        grads_all = store_slot(grads_all, d_conv, slot_clip, is_valid, 1, pixels)
        coef_all = store_slot(coef_all, coef_row[None], slot_clip, is_valid, 0, 1)
        total = jnp.zeros((own_width * lax.axis_size("chan"), pixels), jnp.float32)
        for kernel_pos, (input_oy, input_ox) in enumerate(kernel_offsets):
            weight_rows = lax.dynamic_slice_in_dim(
                weight, kernel_pos * full_width, own_width * lax.axis_size("chan"), 0
            )
            piece_out = lax.dot_general(
                weight_rows, d_conv, (((1,), (0,)), ((), ())), preferred_element_type=jnp.float32
            )
            total = total + shift_grid(piece_out, -input_oy, -input_ox)
        d_input = lax.psum_scatter(total, "chan", scatter_dimension=0, tiled=True)
        returned = (d_input * style_row[:, None]).astype(jnp.bfloat16)
        returned_all = store_slot(returned_all, returned[None], slot_clip, is_valid, 0, 1)
    demod_total = jnp.dot(
        style_sq.T, coef_all, precision=highest, preferred_element_type=jnp.float32
    )
    demod_term = (w_float.reshape(9, full_width, own_width) * demod_total[None]).reshape(
        9 * full_width, own_width
    )
    local_grad = lax.dot_general(
        columns_all, grads_all, (((1,), (1,)), ((), ())), preferred_element_type=jnp.float32
    )
    grad_rows = lax.psum_scatter(
        (local_grad + demod_term).astype(jnp.bfloat16), "dp", scatter_dimension=0, tiled=True
    ).astype(jnp.float32)
    return (grad_rows[None], logits, returned_all[None])


def solution(mesh):
    placed = (
        P("dp", "chan", None),
        P("segment", "dp", None),
        P("segment", "dp", None),
        P("segment", None, "chan"),
        P("segment", "chan"),
        P("segment", "chan"),
        P("segment", None, "chan"),
        P(),
        P(),
        P(),
    )
    return jax.shard_map(
        shards,
        mesh=mesh,
        in_specs=placed,
        out_specs=(P("segment", "dp", "chan"), P("dp"), P("segment", "dp", "chan", None)),
        check_vma=False,
    )
```

profile of v0, /device:TPU:4, one launch (start us, length us, event | category | flops | bytes accessed | tf_op | source)
XLA Modules:
  0.0 444.8 jit_solution(5828866508853112083)
XLA Ops:
  7.3 1.6 constant_dynamic-slice_fusion.15
  9.0 1.6 fusion.192
  10.6 7.3 %all_gather.9 = bf16[512,256]{0,1:T(8,128)(2,1)S(1)} all-gather(bf16[128,256]{0,1:T(8,128)(2,1)S(1)} %fusion.71), channel_id=1, replica_groups=mesh['dp'=32,'segment'=2,'chan'=4] {'chan'}, dimensions={0}, use_global_device_ids=true | all-gather | bytes 327680 | tf_op jit(solution)/shard_map/all_gather | solution.py:93
  17.9 1.2 pad_slice_fusion.40
  19.5 1.6 convert_multiply_fusion
  21.1 2.5 reduce_sum.45
  23.6 1.2 fusion.29
  27.0 1.0 constant_dynamic-update-slice_fusion.2
  28.0 1.0 constant_dynamic-update-slice_fusion.1
  29.0 1.0 constant_dynamic-update-slice_fusion
  30.7 1.5 bitcast_dynamic-update-slice_fusion
  32.2 1.5 fusion.56
  33.6 3.7 collective-permute-start
  38.9 1.0 fusion.28
  39.8 1.6 copy.14
  41.4 1.6 copy.15
  43.9 7.3 %all_gather.10 = bf16[512,256]{0,1:T(8,128)(2,1)S(1)} all-gather(bf16[128,256]{0,1:T(8,128)(2,1)S(1)} %multiply_convert_fusion.7), channel_id=1, replica_groups=mesh['dp'=32,'segment'=2,'chan'=4] {'chan'}, dimensions={0}, use_global_device_ids=true | all-gather | bytes 327680 | tf_op jit(solution)/shard_map/all_gather | solution.py:93
  52.1 2.8 fusion.66
  55.1 1.3 collective-permute-start.1
  56.6 2.0 collective-permute-done.1
  58.6 7.3 %all_gather.11 = bf16[512,256]{0,1:T(8,128)(2,1)S(1)} all-gather(bf16[128,256]{0,1:T(8,128)(2,1)S(1)} %multiply_convert_fusion.6), channel_id=1, replica_groups=mesh['dp'=32,'segment'=2,'chan'=4] {'chan'}, dimensions={0}, use_global_device_ids=true | all-gather | bytes 327680 | tf_op jit(solution)/shard_map/all_gather | solution.py:93
  66.5 1.4 copy-done.4
  67.9 2.5 fusion.65
  70.7 14.6 %psum.7 = f32[2,3,256]{2,1,0:T(4,128)} all-reduce(f32[2,3,256]{2,1,0:T(4,128)S(1)} %fusion.26), channel_id=1, replica_groups=mesh['dp'=32,'segment'=2,'chan'=4] {'segment','chan'}, use_global_device_ids=true, to_apply=%region_1.2 | all-reduce | flops 1536 | bytes 12288 | tf_op jit(solution)/shard_map/psum | solution.py:112
  85.2 1.6 fusion.41
  86.9 1.3 divide_add_fusion
  90.1 1.1 fusion.167
  93.6 1.1 fusion.8
  94.7 35.7 %reduce-scatter.5.cloned.1.call-done = f32[128,256]{0,1:T(8,128)} async-done(((f32[512,256]{0,1:T(8,128)}), f32[128,256]{0,1:T(8,128)}) %reduce-scatter.5.cloned.1.call-update) | async-done | bytes 131088 | tf_op jit(solution)/shard_map/reduce_scatter | solution.py:158
  131.1 1.6 bitcast_dynamic-update-slice_fusion.2
  132.7 1.5 collective-permute-start.2
  134.1 2.4 broadcast_in_dim.35
  136.6 1.8 select_dynamic-update-slice_fusion.2
  139.1 1.8 select_dynamic-update-slice_fusion.4
  143.2 1.1 fusion.12
  145.1 3.7 select_dynamic-update-slice_fusion.1
  148.8 30.0 %reduce-scatter.7.cloned.1.call-done = f32[128,256]{0,1:T(8,128)} async-done(((f32[512,256]{0,1:T(8,128)}), f32[128,256]{0,1:T(8,128)}) %reduce-scatter.7.cloned.1.call-update) | async-done | bytes 131088 | tf_op jit(solution)/shard_map/reduce_scatter | solution.py:158
  178.8 1.6 fusion.168
  180.4 1.4 collective-permute-start.3
  181.8 3.6 select_dynamic-update-slice_fusion
  185.4 1.2 collective-permute-done.3
  186.7 1.0 select_dynamic-update-slice_fusion.3
  190.1 1.1 fusion.16
  191.2 1.1 fusion.72
  193.3 4.9 %fusion = bf16[4608,128]{1,0:T(8,128)(2,1)} fusion(f32[4608,128]{1,0:T(8,128)S(1)} %bitcast_multiply_fusion, bf16[4608,512]{0,1:T(8,128)(2,1)} %select_dynamic-update-slice_fusion, bf16[128,512]{0,1:T(8,128)(2,1)S(1)} %get-tuple-element.13), kind=kOutput, calls=%fused_computation.1 | convolution fusion | flops 605159424 | bytes 8388608 | tf_op jit(solution)/shard_map/dot_general | solution.py:167
  199.2 26.3 %reduce-scatter.11.cloned.1.call-done = f32[128,256]{0,1:T(8,128)} async-done(((f32[512,256]{0,1:T(8,128)}), f32[128,256]{0,1:T(8,128)}) %reduce-scatter.11.cloned.1.call-update) | async-done | bytes 131088 | tf_op jit(solution)/shard_map/reduce_scatter | solution.py:158
  227.1 209.8 %reduce-scatter.9.cloned.1.call-done = bf16[144,128]{1,0:T(8,128)(2,1)} async-done(((bf16[4608,128]{1,0:T(8,128)(2,1)}), bf16[144,128]{1,0:T(8,128)(2,1)}) %reduce-scatter.9.cloned.1.call-update) | async-done | bytes 36880 | tf_op jit(solution)/shard_map/reduce_scatter | solution.py:170
  436.9 1.4 bitcast_convert_fusion
  (179 shorter events, 22.3 us)
Async XLA Ops:
  7.2 78.1 %copy-start = (f32[3,256]{1,0:T(4,128)S(1)}, f32[3,256]{1,0:T(4,128)}, u32[]{:S(2)}) copy-start(f32[3,256]{1,0:T(4,128)} %param.17) | copy-start | bytes 9220
  7.2 123.2 %reduce-scatter.5.cloned.1.call-start = ((), (), s32[]{:S(2)}) async-start(), calls=%async_computation.4 | async-start | bytes 655360 | tf_op jit(solution)/shard_map/reduce_scatter | solution.py:158
  17.9 1.6 copy-start.1
  19.5 4.1 copy-start.13
  19.5 5.9 %copy-start.29 = (f32[1,2,256]{2,1,0:T(2,128)S(1)}, f32[1,2,256]{2,1,0:T(2,128)}, u32[]{:S(2)}) copy-start(f32[1,2,256]{2,1,0:T(2,128)} %param.12) | copy-start | bytes 6148
  24.8 4.2 copy-start.15
  28.9 3.2 copy-start.18
  29.0 3.2 copy-start.20
  30.0 8.1 %copy-start.25 = (f32[1,1,256]{2,1,0:T(1,128)S(1)}, f32[1,1,256]{2,1,0:T(1,128)}, u32[]{:S(2)}) copy-start(f32[1,1,256]{2,1,0:T(1,128)} %get-tuple-element.59) | copy-start | bytes 3076
  30.0 8.1 %copy-start.28 = (f32[128]{0:T(128)S(1)}, f32[128]{0:T(128)}, u32[]{:S(2)}) copy-start(f32[128]{0:T(128)} %get-tuple-element.66) | copy-start | bytes 1540
  30.0 8.9 %copy-start.22 = (bf16[1,3,128]{2,1,0:T(4,128)(2,1)S(1)}, bf16[1,3,128]{2,1,0:T(4,128)(2,1)}, u32[]{:S(2)}) copy-start(bf16[1,3,128]{2,1,0:T(4,128)(2,1)} %param.16) | copy-start | bytes 2308
  33.6 9.3 %collective-permute-start = (bf16[128,256]{0,1:T(8,128)(2,1)}, bf16[128,256]{0,1:T(8,128)(2,1)}, u32[]{:S(2)}, u32[]{:S(2)}) collective-permute-start(bf16[128,256]{0,1:T(8,128)(2,1)} %fusion.56), channel_id=1, source_target_pairs={{0,4},{1,5},{2,6},{3,7},{8,12},{9,13},{10,14},{11,15},{16,20},{17,... | collective-permute-start | bytes 196616 | tf_op jit(solution)/shard_map/ppermute | solution.py:16
  51.5 0.7 copy-start.19
  51.5 0.7 copy-start.21
  51.5 0.7 copy-start.26
  51.7 4.7 %copy-start.23 = (bf16[1,3,128]{2,1,0:T(4,128)(2,1)S(1)}, bf16[1,3,128]{2,1,0:T(4,128)(2,1)}, u32[]{:S(2)}) copy-start(bf16[1,3,128]{2,1,0:T(4,128)(2,1)} %param.16) | copy-start | bytes 2308
  51.7 14.2 %copy-start.2 = (bf16[4608,256]{0,1:T(8,128)(2,1)}, bf16[4608,256]{0,1:T(8,128)(2,1)S(1)}, u32[]{:S(2)}) copy-start(bf16[4608,256]{0,1:T(8,128)(2,1)S(1)} %constant_dynamic-update-slice_fusion.9) | copy-start | bytes 7077892
  51.8 6.8 %copy-start.12 = (bf16[1,128,256]{1,2,0:T(8,128)(2,1)S(1)}, bf16[1,128,256]{1,2,0:T(8,128)(2,1)}, u32[]{:S(2)}) copy-start(bf16[1,128,256]{1,2,0:T(8,128)(2,1)} %copy.15) | copy-start | bytes 196612
  51.8 6.8 %copy-start.36 = (f32[128]{0:T(128)S(1)}, f32[128]{0:T(128)}, u32[]{:S(2)}) copy-start(f32[128]{0:T(128)} %get-tuple-element.54) | copy-start | bytes 1540
  55.1 3.4 collective-permute-start.1
  66.2 1.7 copy-start.17
  66.2 1.7 copy-start.30
  66.5 1.4 copy-start.4
  70.4 19.3 %copy-start.24 = (bf16[1,3,128]{2,1,0:T(4,128)(2,1)S(1)}, bf16[1,3,128]{2,1,0:T(4,128)(2,1)}, u32[]{:S(2)}) copy-start(bf16[1,3,128]{2,1,0:T(4,128)(2,1)} %param.16) | copy-start | bytes 2308
  85.2 4.9 %copy-start.27 = (f32[128]{0:T(128)S(1)}, f32[128]{0:T(128)}, u32[]{:S(2)}) copy-start(f32[128]{0:T(128)} %get-tuple-element.63) | copy-start | bytes 1540
  90.1 2.5 copy-start.5
  91.2 1.7 copy-start.7
  91.2 1.7 copy-start.9
  93.6 37.5 %copy-start.35 = (f32[128]{0:T(128)S(1)}, f32[128]{0:T(128)}, u32[]{:S(2)}) copy-start(f32[128]{0:T(128)} %get-tuple-element.53) | copy-start | bytes 1540
  94.6 84.2 %reduce-scatter.7.cloned.1.call-start = ((), (), s32[]{:S(2)}) async-start(), calls=%async_computation.5 | async-start | bytes 655360 | tf_op jit(solution)/shard_map/reduce_scatter | solution.py:158
  132.7 6.5 %collective-permute-start.2 = (bf16[128,256]{0,1:T(8,128)(2,1)}, bf16[128,256]{0,1:T(8,128)(2,1)}, u32[]{:S(2)}, u32[]{:S(2)}) collective-permute-start(bf16[128,256]{0,1:T(8,128)(2,1)} %get-tuple-element.12), channel_id=1, source_target_pairs={{4,0},{5,1},{6,2},{7,3},{12,8},{13,9},{14,10},{15,11},{20,16},{21,... | collective-permute-start | bytes 196616 | tf_op jit(solution)/shard_map/ppermute | solution.py:16
  136.6 2.6 copy-start.34
  143.2 1.9 copy-start.3
  144.3 34.5 %copy-start.32 = (f32[128]{0:T(128)S(1)}, f32[128]{0:T(128)}, u32[]{:S(2)}) copy-start(f32[128]{0:T(128)} %get-tuple-element.57) | copy-start | bytes 1540
  144.3 81.1 %reduce-scatter.11.cloned.1.call-start = ((), (), s32[]{:S(2)}) async-start(), calls=%async_computation.7 | async-start | bytes 655360 | tf_op jit(solution)/shard_map/reduce_scatter | solution.py:158
  180.4 6.3 %copy-start.6 = (f32[2,256,128]{2,1,0:T(8,128)S(1)}, f32[2,256,128]{2,1,0:T(8,128)}, u32[]{:S(2)}) copy-start(f32[2,256,128]{2,1,0:T(8,128)} %copy-done.5) | copy-start | bytes 786436
  180.4 6.3 %copy-start.8 = (bf16[128,512]{0,1:T(8,128)(2,1)S(1)}, bf16[128,512]{0,1:T(8,128)(2,1)}, u32[]{:S(2)}) copy-start(bf16[128,512]{0,1:T(8,128)(2,1)} %get-tuple-element.16) | copy-start | bytes 393220
  180.4 6.3 %copy-start.33 = (f32[128]{0:T(128)S(1)}, f32[128]{0:T(128)}, u32[]{:S(2)}) copy-start(f32[128]{0:T(128)} %get-tuple-element.61) | copy-start | bytes 1540
  180.4 6.3 %collective-permute-start.3 = (bf16[128,256]{0,1:T(8,128)(2,1)S(1)}, bf16[128,256]{0,1:T(8,128)(2,1)S(1)}, u32[]{:S(2)}, u32[]{:S(2)}) collective-permute-start(bf16[128,256]{0,1:T(8,128)(2,1)S(1)} %get-tuple-element.10), channel_id=1, source_target_pairs={{4,0},{5,1},{6,2},{7,3},{12,8},{13,9},{14,10},{15,11},{20,16},{21,... | collective-permute-start | bytes 196616 | tf_op jit(solution)/shard_map/ppermute | solution.py:16
  190.0 1.2 copy-start.10
  190.0 1.2 copy-start.11
  190.0 2.3 copy-start.16
  190.0 2.5 copy-start.14
  191.2 245.7 %reduce-scatter.9.cloned.1.call-start = ((), (), s32[]{:S(2)}) async-start(), calls=%async_computation.6 | async-start | bytes 1216512 | tf_op jit(solution)/shard_map/reduce_scatter | solution.py:170
  193.3 32.1 %copy-start.31 = (f32[128]{0:T(128)S(1)}, f32[128]{0:T(128)}, u32[]{:S(2)}) copy-start(f32[128]{0:T(128)} %get-tuple-element.52) | copy-start | bytes 1540
Sparse Core Ops, SparseCore 0:
  94.8 35.6 reduce-scatter.4
  144.4 34.3 reduce-scatter.6
  191.3 34.1 reduce-scatter.10
  229.1 207.7 reduce-scatter.8
where the time goes:
time: 446 us; the launch traced here: 445 us
  waiting for transfers between devices  306 us (69%)
  blocking collectives  36.5 us (8%)
  other arithmetic  28.7 us (6%)
  matrix products  27.4 us (6%)
  local copies, waits for them, and re-layouts  23.6 us (5%)
  between operations  14.8 us (3%)
  starting transfers between devices  8.04 us (2%)
    reduce_scatter x1, waiting for transfers between devices, shards(): lax.psum_scatter((local_grad + demod_term).astype(jnp.bfloat16), 'dp', sc...  210 us
    reduce_scatter x3, waiting for transfers between devices, shards(): d_input = lax.psum_scatter(total, 'chan', scatter_dimension=0, tiled=True)  92 us
    all_gather x3, blocking collectives, shards(): gathered = lax.all_gather(modulated, 'chan', axis=0, tiled=True)  21.9 us
    dynamic_update_slice x10, other arithmetic, store_slot(): lax.dynamic_update_slice_in_dim(buffer, jnp.where(is_valid, item, previou...  17.9 us
    psum x1, blocking collectives, shards(): images = lax.psum(image_part, ('segment', 'chan'))  14.6 us
  transfers between devices with their start and end apart: 8, of which 7 were waited for; matrix products, arithmetic and copies ran while one was open for 6% of the time, Pallas kernels for 0%

commit v1 on v0

--- a/solution.py
+++ b/solution.py
@@ -90,7 +90,9 @@
         demod_row = lax.dynamic_index_in_dim(demods, slot_clip, 0, keepdims=False)
         noise_row = lax.dynamic_index_in_dim(noises, slot_clip, 0, keepdims=False)
         modulated = (inputs.astype(jnp.float32) * style_row[:, None]).astype(jnp.bfloat16)
-        gathered = lax.all_gather(modulated, "chan", axis=0, tiled=True)
+        gathered = jnp.concatenate(
+            lax.all_to_all(jnp.stack([modulated] * lax.axis_size("chan")), "chan", 0, 0), axis=0
+        )
         columns = jnp.concatenate(
             [shift_grid(gathered, oy, ox) for oy, ox in kernel_offsets], axis=0
         )

time: 446 us -> 460 us (1.031)
  blocking collectives: 36.5 us -> 16.2 us
  starting transfers between devices: 8.04 us -> 27.3 us
  local copies, waits for them, and re-layouts: 23.6 us -> 34.4 us
  waiting for transfers between devices: 306 us -> 314 us
    all_gather x3 -> x0, blocking collectives: 21.9 us -> none  [shards(): gathered = lax.all_gather(modulated, 'chan', axis=0, tiled=True)]
    all_to_all x0 -> x3, starting transfers between devices: none -> 18.7 us  [shards(): lax.all_to_all(jnp.stack([modulated] * lax.axis_size('chan')), 'chan', 0, 0)]
    all_to_all x0 -> x3, waiting for transfers between devices: none -> 6.88 us  [shards(): lax.all_to_all(jnp.stack([modulated] * lax.axis_size('chan')), 'chan', 0, 0)]
    another operation x2 -> x9, local copies, waits for them, and re-layouts: 1.45 us -> 7.39 us  [the longest x3 3.64 us: shift_grid(): planes = values.reshape(leading + (RES, RES))]
    unnamed x101 -> x120, local copies, waits for them, and re-layouts: 8.09 us -> 9.29 us
  transfers between devices with their start and end apart: 8 -> 11, of which waited for: 7 -> 10; matrix products, arithmetic and copies ran while one was open for 6% -> 6% of each run, Pallas kernels for 0% -> 0%
where the time goes in v1:
time: 460 us; the launch traced here: 459 us
  waiting for transfers between devices  314 us (68%)
  local copies, waits for them, and re-layouts  34.4 us (7%)
  starting transfers between devices  27.3 us (6%)
  matrix products  27.1 us (6%)
  other arithmetic  25.5 us (6%)
  blocking collectives  16.2 us (4%)
  between operations  15 us (3%)
    reduce_scatter x1, waiting for transfers between devices, shards(): lax.psum_scatter((local_grad + demod_term).astype(jnp.bfloat16), 'dp', sc...  210 us
    reduce_scatter x3, waiting for transfers between devices, shards(): d_input = lax.psum_scatter(total, 'chan', scatter_dimension=0, tiled=True)  90.9 us
    all_to_all x3, starting transfers between devices, shards(): lax.all_to_all(jnp.stack([modulated] * lax.axis_size('chan')), 'chan', 0, 0)  18.7 us
    dynamic_update_slice x10, other arithmetic, store_slot(): lax.dynamic_update_slice_in_dim(buffer, jnp.where(is_valid, item, previou...  16.9 us
    psum x1, blocking collectives, shards(): images = lax.psum(image_part, ('segment', 'chan'))  16.2 us
    unnamed x120, local copies, waits for them, and re-layouts  9.29 us
  transfers between devices with their start and end apart: 11, of which 10 were waited for; matrix products, arithmetic and copies ran while one was open for 6% of the time, Pallas kernels for 0%

profile of v1, /device:TPU:4, one launch (start us, length us, event | category | flops | bytes accessed | tf_op | source)
XLA Modules:
  0.0 459.0 jit_solution(5838010167549405489)
XLA Ops:
  7.2 1.6 fusion.192
  10.6 5.6 %all-to-all-start = ((bf16[4,128,256]{1,2,0:T(8,128)(2,1)}), bf16[4,128,256]{1,2,0:T(8,128)(2,1)S(1)}, u32[]{:S(2)}, u32[]{:S(2)}) async-start(bf16[4,128,256]{1,2,0:T(8,128)(2,1)} %stack.9), calls=%async_computation | async-start | bytes 524288 | tf_op jit(solution)/shard_map/all_to_all | solution.py:94
  16.2 1.5 convert_multiply_fusion
  19.3 1.3 all-to-all-done
  21.4 1.1 bitcast_dynamic-update-slice_fusion.2
  23.3 1.4 bitcast_dynamic-update-slice_fusion.3
  26.2 2.9 collective-permute-start
  29.8 1.6 copy.25
  31.4 1.6 copy.28
  34.6 6.5 %all-to-all-start.1 = ((bf16[4,128,256]{1,2,0:T(8,128)(2,1)}), bf16[4,128,256]{1,2,0:T(8,128)(2,1)}, u32[]{:S(2)}, u32[]{:S(2)}) async-start(bf16[4,128,256]{1,2,0:T(8,128)(2,1)} %stack.10), calls=%async_computation.1 | async-start | bytes 524288 | tf_op jit(solution)/shard_map/all_to_all | solution.py:94
  41.8 1.7 bitcast_dynamic-update-slice_fusion.4
  43.5 2.1 all-to-all-done.1
  45.6 1.9 copy.26
  47.4 1.7 reshape_reshape.7
  49.2 2.8 pad_slice_fusion.32
  53.3 1.4 copy-done.3
  54.6 2.5 fusion.66
  57.3 2.7 collective-permute-start.1
  62.6 6.5 %all-to-all-start.2 = ((bf16[4,128,256]{1,2,0:T(8,128)(2,1)}), bf16[4,128,256]{1,2,0:T(8,128)(2,1)}, u32[]{:S(2)}, u32[]{:S(2)}) async-start(bf16[4,128,256]{1,2,0:T(8,128)(2,1)} %stack.11), calls=%async_computation.2 | async-start | bytes 524288 | tf_op jit(solution)/shard_map/all_to_all | solution.py:94
  70.2 3.5 all-to-all-done.2
  73.7 1.8 copy.29
  75.5 1.8 reshape_reshape.8
  77.3 3.0 pad_slice_fusion.24
  81.6 1.5 copy-done.5
  83.1 2.5 fusion.65
  85.9 16.2 %psum.7 = f32[2,3,256]{2,1,0:T(4,128)} all-reduce(f32[2,3,256]{2,1,0:T(4,128)S(1)} %fusion.26), channel_id=1, replica_groups=mesh['dp'=32,'segment'=2,'chan'=4] {'segment','chan'}, use_global_device_ids=true, to_apply=%region_1.2 | all-reduce | flops 1536 | bytes 12288 | tf_op jit(solution)/shard_map/psum | solution.py:114
  102.0 1.6 fusion.41
  103.7 1.3 divide_add_fusion
  106.9 1.1 fusion.167
  110.3 1.1 fusion.8
  111.5 35.5 %reduce-scatter.5.cloned.1.call-done = f32[128,256]{0,1:T(8,128)} async-done(((f32[512,256]{0,1:T(8,128)}), f32[128,256]{0,1:T(8,128)}) %reduce-scatter.5.cloned.1.call-update) | async-done | bytes 131088 | tf_op jit(solution)/shard_map/reduce_scatter | solution.py:160
  148.6 1.5 collective-permute-start.2
  151.0 3.8 collective-permute-done.2
  154.8 1.7 select_dynamic-update-slice_fusion.4
  158.8 1.1 fusion.12
  160.7 3.8 select_dynamic-update-slice_fusion.1
  164.5 28.2 %reduce-scatter.7.cloned.1.call-done = f32[128,256]{0,1:T(8,128)} async-done(((f32[512,256]{0,1:T(8,128)}), f32[128,256]{0,1:T(8,128)}) %reduce-scatter.7.cloned.1.call-update) | async-done | bytes 131088 | tf_op jit(solution)/shard_map/reduce_scatter | solution.py:160
  192.6 1.6 fusion.168
  194.2 1.4 collective-permute-start.3
  195.6 3.7 select_dynamic-update-slice_fusion
  199.3 1.2 collective-permute-done.3
  200.5 1.0 select_dynamic-update-slice_fusion.3
  203.9 1.1 fusion.16
  205.0 1.1 fusion.71
  207.2 4.9 %fusion = bf16[4608,128]{1,0:T(8,128)(2,1)} fusion(f32[4608,128]{1,0:T(8,128)S(1)} %bitcast_multiply_fusion, bf16[4608,512]{0,1:T(8,128)(2,1)} %select_dynamic-update-slice_fusion, bf16[128,512]{0,1:T(8,128)(2,1)S(1)} %get-tuple-element.19), kind=kOutput, calls=%fused_computation.1 | convolution fusion | flops 605159424 | bytes 8388608 | tf_op jit(solution)/shard_map/dot_general | solution.py:169
  212.1 27.2 %reduce-scatter.11.cloned.1.call-done = f32[128,256]{0,1:T(8,128)} async-done(((f32[512,256]{0,1:T(8,128)}), f32[128,256]{0,1:T(8,128)}) %reduce-scatter.11.cloned.1.call-update) | async-done | bytes 131088 | tf_op jit(solution)/shard_map/reduce_scatter | solution.py:160
  241.1 210.0 %reduce-scatter.9.cloned.1.call-done = bf16[144,128]{1,0:T(8,128)(2,1)} async-done(((bf16[4608,128]{1,0:T(8,128)(2,1)}), bf16[144,128]{1,0:T(8,128)(2,1)}) %reduce-scatter.9.cloned.1.call-update) | async-done | bytes 36880 | tf_op jit(solution)/shard_map/reduce_scatter | solution.py:172
  451.0 1.4 bitcast_convert_fusion
  (211 shorter events, 30.5 us)
Async XLA Ops:
  7.2 94.9 %copy-start = (f32[3,256]{1,0:T(4,128)S(1)}, f32[3,256]{1,0:T(4,128)}, u32[]{:S(2)}) copy-start(f32[3,256]{1,0:T(4,128)} %param.17) | copy-start | bytes 9220
  10.6 10.0 %all-to-all-start = ((bf16[4,128,256]{1,2,0:T(8,128)(2,1)}), bf16[4,128,256]{1,2,0:T(8,128)(2,1)S(1)}, u32[]{:S(2)}, u32[]{:S(2)}) async-start(bf16[4,128,256]{1,2,0:T(8,128)(2,1)} %stack.9), calls=%async_computation | async-start | bytes 524288 | tf_op jit(solution)/shard_map/all_to_all | solution.py:94
  16.2 2.5 copy-start.39
  18.0 3.1 copy-start.24
  21.3 2.0 copy-start.1
  22.5 2.9 copy-start.27
  22.5 2.9 copy-start.29
  22.5 2.9 copy-start.35
  22.5 2.9 copy-start.38
  22.5 6.6 %copy-start.20 = (bf16[2,128,256]{2,1,0:T(8,128)(2,1)S(1)}, bf16[2,128,256]{2,1,0:T(8,128)(2,1)}, u32[]{:S(2)}) copy-start(bf16[2,128,256]{2,1,0:T(8,128)(2,1)} %param.10) | copy-start | bytes 393220
  26.2 6.7 %collective-permute-start = (bf16[128,256]{0,1:T(8,128)(2,1)}, bf16[128,256]{0,1:T(8,128)(2,1)}, u32[]{:S(2)}, u32[]{:S(2)}) collective-permute-start(bf16[128,256]{0,1:T(8,128)(2,1)} %fusion.56), channel_id=1, source_target_pairs={{0,4},{1,5},{2,6},{3,7},{8,12},{9,13},{10,14},{11,15},{16,20},{17,... | collective-permute-start | bytes 196616 | tf_op jit(solution)/shard_map/ppermute | solution.py:16
  34.6 11.0 %all-to-all-start.1 = ((bf16[4,128,256]{1,2,0:T(8,128)(2,1)}), bf16[4,128,256]{1,2,0:T(8,128)(2,1)}, u32[]{:S(2)}, u32[]{:S(2)}) async-start(bf16[4,128,256]{1,2,0:T(8,128)(2,1)} %stack.10), calls=%async_computation.1 | async-start | bytes 524288 | tf_op jit(solution)/shard_map/all_to_all | solution.py:94
  52.0 2.6 copy-start.30
  52.0 2.6 copy-start.36
  53.2 6.8 %copy-start.32 = (bf16[1,3,128]{2,1,0:T(4,128)(2,1)S(1)}, bf16[1,3,128]{2,1,0:T(4,128)(2,1)}, u32[]{:S(2)}) copy-start(bf16[1,3,128]{2,1,0:T(4,128)(2,1)} %param.16) | copy-start | bytes 2308
  53.2 8.7 %copy-start.21 = (bf16[1,128,256]{1,2,0:T(8,128)(2,1)S(1)}, bf16[1,128,256]{1,2,0:T(8,128)(2,1)}, u32[]{:S(2)}) copy-start(bf16[1,128,256]{1,2,0:T(8,128)(2,1)} %copy.28) | copy-start | bytes 196612
  53.2 8.6 %copy-start.46 = (f32[128]{0:T(128)S(1)}, f32[128]{0:T(128)}, u32[]{:S(2)}) copy-start(f32[128]{0:T(128)} %get-tuple-element.59) | copy-start | bytes 1540
  57.3 4.6 %copy-start.22 = (bf16[128,256]{0,1:T(8,128)(2,1)}, bf16[128,256]{0,1:T(8,128)(2,1)S(1)}, u32[]{:S(2)}) copy-start(bf16[128,256]{0,1:T(8,128)(2,1)S(1)} %fusion.60) | copy-start | bytes 196612
  57.3 4.6 collective-permute-start.1
  62.6 11.0 %all-to-all-start.2 = ((bf16[4,128,256]{1,2,0:T(8,128)(2,1)}), bf16[4,128,256]{1,2,0:T(8,128)(2,1)}, u32[]{:S(2)}, u32[]{:S(2)}) async-start(bf16[4,128,256]{1,2,0:T(8,128)(2,1)} %stack.11), calls=%async_computation.2 | async-start | bytes 524288 | tf_op jit(solution)/shard_map/all_to_all | solution.py:94
  69.2 77.8 %reduce-scatter.5.cloned.1.call-start = ((), (), s32[]{:S(2)}) async-start(), calls=%async_computation.7 | async-start | bytes 655360 | tf_op jit(solution)/shard_map/reduce_scatter | solution.py:160
  80.4 2.7 copy-start.26
  80.4 2.7 copy-start.28
  80.4 2.7 copy-start.31
  80.4 2.7 copy-start.40
  81.6 4.0 copy-start.33
  102.0 4.4 copy-start.34
  102.0 4.9 %copy-start.37 = (f32[128]{0:T(128)S(1)}, f32[128]{0:T(128)}, u32[]{:S(2)}) copy-start(f32[128]{0:T(128)} %get-tuple-element.68) | copy-start | bytes 1540
  106.8 2.5 copy-start.7
  108.0 1.7 copy-start.15
  110.3 36.7 %copy-start.44 = (f32[128]{0:T(128)S(1)}, f32[128]{0:T(128)}, u32[]{:S(2)}) copy-start(f32[128]{0:T(128)} %get-tuple-element.58) | copy-start | bytes 1540
  111.4 81.2 %reduce-scatter.7.cloned.1.call-start = ((), (), s32[]{:S(2)}) async-start(), calls=%async_computation.8 | async-start | bytes 655360 | tf_op jit(solution)/shard_map/reduce_scatter | solution.py:160
  148.6 6.1 %collective-permute-start.2 = (bf16[128,256]{0,1:T(8,128)(2,1)S(1)}, bf16[128,256]{0,1:T(8,128)(2,1)S(1)}, u32[]{:S(2)}, u32[]{:S(2)}) collective-permute-start(bf16[128,256]{0,1:T(8,128)(2,1)S(1)} %get-tuple-element.18), channel_id=1, source_target_pairs={{4,0},{5,1},{6,2},{7,3},{12,8},{13,9},{14,10},{15,11},{20,16},{21,... | collective-permute-start | bytes 196616 | tf_op jit(solution)/shard_map/ppermute | solution.py:16
  150.4 4.4 copy-start.8
  150.4 4.4 copy-start.11
  150.4 4.4 copy-start.45
  151.0 6.8 %copy-start.2 = (bf16[4608,512]{0,1:T(8,128)(2,1)}, bf16[4608,512]{0,1:T(8,128)(2,1)S(1)}, u32[]{:S(2)}) copy-start(bf16[4608,512]{0,1:T(8,128)(2,1)S(1)} %select_dynamic-update-slice_fusion.2) | copy-start | bytes 14155780
  158.8 1.9 copy-start.4
  159.9 32.7 %copy-start.42 = (f32[128]{0:T(128)S(1)}, f32[128]{0:T(128)}, u32[]{:S(2)}) copy-start(f32[128]{0:T(128)} %get-tuple-element.62) | copy-start | bytes 1540
  159.9 79.4 %reduce-scatter.11.cloned.1.call-start = ((), (), s32[]{:S(2)}) async-start(), calls=%async_computation.10 | async-start | bytes 655360 | tf_op jit(solution)/shard_map/reduce_scatter | solution.py:160
  194.2 6.3 %copy-start.9 = (f32[2,256,128]{2,1,0:T(8,128)S(1)}, f32[2,256,128]{2,1,0:T(8,128)}, u32[]{:S(2)}) copy-start(f32[2,256,128]{2,1,0:T(8,128)} %copy-done.7) | copy-start | bytes 786436
  194.2 6.3 %copy-start.13 = (bf16[128,512]{0,1:T(8,128)(2,1)S(1)}, bf16[128,512]{0,1:T(8,128)(2,1)}, u32[]{:S(2)}) copy-start(bf16[128,512]{0,1:T(8,128)(2,1)} %copy-done.12) | copy-start | bytes 393220
  194.2 6.3 %copy-start.43 = (f32[128]{0:T(128)S(1)}, f32[128]{0:T(128)}, u32[]{:S(2)}) copy-start(f32[128]{0:T(128)} %get-tuple-element.66) | copy-start | bytes 1540
  194.2 6.3 %collective-permute-start.3 = (bf16[128,256]{0,1:T(8,128)(2,1)S(1)}, bf16[128,256]{0,1:T(8,128)(2,1)S(1)}, u32[]{:S(2)}, u32[]{:S(2)}) collective-permute-start(bf16[128,256]{0,1:T(8,128)(2,1)S(1)} %get-tuple-element.16), channel_id=1, source_target_pairs={{4,0},{5,1},{6,2},{7,3},{12,8},{13,9},{14,10},{15,11},{20,16},{21,... | collective-permute-start | bytes 196616 | tf_op jit(solution)/shard_map/ppermute | solution.py:16
  203.9 2.3 copy-start.25
  205.0 246.1 %reduce-scatter.9.cloned.1.call-start = ((), (), s32[]{:S(2)}) async-start(), calls=%async_computation.9 | async-start | bytes 1216512 | tf_op jit(solution)/shard_map/reduce_scatter | solution.py:172
  207.1 5.0 %copy-start.18 = (bf16[2,128,256]{1,2,0:T(8,128)(2,1)S(1)}, bf16[2,128,256]{1,2,0:T(8,128)(2,1)}, u32[]{:S(2)}) copy-start(bf16[2,128,256]{1,2,0:T(8,128)(2,1)} %get-tuple-element.15) | copy-start | bytes 393220
  207.1 32.2 %copy-start.41 = (f32[128]{0:T(128)S(1)}, f32[128]{0:T(128)}, u32[]{:S(2)}) copy-start(f32[128]{0:T(128)} %get-tuple-element.57) | copy-start | bytes 1540
  (10 other events, 12.1 us)
Sparse Core Ops, SparseCore 0:
  111.6 35.3 reduce-scatter.4
  160.0 32.5 reduce-scatter.6
  205.1 34.2 reduce-scatter.10
  243.0 207.9 reduce-scatter.8
